TPU v7x, 32 devices: a whole 2x2x4 slice. The times are simulated.
32 devices in a mesh: dp: 4 (over x, core), mp: 8 (over z, y).
Axes of the slice: x: 2, y: 2, z: 4, core: 2. Of those that a mesh axis runs over, the one named last changes fastest.
Arguments:
- block_input: bfloat16 [4096, 2048], P(('dp', 'mp')), may hold values from -6 to 6
- out_cotangent: bfloat16 [4096, 2048], P(('dp', 'mp')), may hold values from -6 to 6
- segments: int32 [4, 1024], P('dp'), may hold values from 0 to 3, never falling along the last dimension, each value on 1 to 512 neighbouring positions
- domain_tags: int32 [4], P('dp'), may hold values from 0 to 7
- counts: int32 [8], replicated, may hold values from 1 to 4
- attn_gain: float32 [2048], replicated, may hold values from 0.5 to 1.5
- mlp_gain: float32 [2048], replicated, may hold values from 0.5 to 1.5
- norm_gain: float32 [2048], P('mp'), may hold values from 0.5 to 1.5
- bound_table: float32 [24, 2048], P(None, 'mp'), may hold values from -4 to 4
- w_input: bfloat16 [2048, 2048], P(None, 'mp'), may hold values from -0.125 to 0.125
- w_forget: bfloat16 [2048, 2048], P(None, 'mp'), may hold values from -0.125 to 0.125
- w_gate_mix: bfloat16 [2048, 2048], P(None, 'mp'), may hold values from -0.125 to 0.125
- w_out: bfloat16 [2048, 2048], P('mp'), may hold values from -0.1875 to 0.1875
- w_glu_gate: bfloat16 [2048, 5632], P(None, 'mp'), may hold values from -0.125 to 0.125
- w_glu_up: bfloat16 [2048, 5632], P(None, 'mp'), may hold values from -0.125 to 0.125
- w_glu_down: bfloat16 [5632, 2048], P('mp'), may hold values from -0.109375 to 0.109375
Outputs:
- result: bfloat16 [4096, 2048], P(('dp', 'mp'))
- grad_block_input: float32 [4096, 2048], P(('dp', 'mp'))
- grad_attn_gain: float32 [2048], replicated
- grad_mlp_gain: float32 [2048], replicated
- grad_norm_gain: float32 [2048], replicated
- grad_bound_table: float32 [24, 2048], replicated
- grad_input: float32 [2048, 2048], P('dp', 'mp')
- grad_forget: float32 [2048, 2048], P('dp', 'mp')
- grad_gate_mix: float32 [2048, 2048], P('dp', 'mp')
- grad_out: float32 [2048, 2048], P('mp', 'dp')
- grad_glu_gate: float32 [2048, 5632], P('dp', 'mp')
- grad_glu_up: float32 [2048, 5632], P('dp', 'mp')
- grad_glu_down: float32 [5632, 2048], P('mp', 'dp')
Inputs may be any that keep to these rules, and one draw needn't show every extreme that they name: `segments`: along each row the document ids never fall; each document has at least one position.
All inputs are finite; a program needn't handle non-finite values.
Results may differ from a plain program's by a relative error of at most 0.022.
Values may be sent and summed in bfloat16 or wider, within the bound.
No kernel may reach another device: no remote copies, remote signals or barrier semaphores. Data moves between devices by JAX's collectives and lax.ppermute only.
A program may use at most 320 MiB of HBM per device.

v0:
```python
import jax
import jax.numpy as jnp
from jax import lax
from jax.sharding import PartitionSpec as P

NLAYER = 24
LAYER = 20
LEN = 1024
BLK = 128
NDOM = 8
EPS = 1e-06
HIGH = lax.Precision.HIGHEST


def inverse_rms(rows):
    return lax.rsqrt(jnp.mean(rows * rows, axis=1, keepdims=True) + EPS)


def silu_slope(value):
    sig = jax.nn.sigmoid(value)
    return sig * (1.0 + value * (1.0 - sig))


def norm_back(grad_normed, rows, inverse, gain):
    scaled = grad_normed * gain
    unit = rows * inverse
    back = inverse * (scaled - unit * jnp.mean(scaled * unit, axis=1, keepdims=True))
    return (back, jnp.sum(grad_normed * unit, axis=0))


def block_terms(log_blk, reset_blk, lower):
    cum_log = jnp.einsum("csu,tu->cst", log_blk, lower, precision=HIGH)
    cum_reset = jnp.einsum("su,tu->st", reset_blk, lower, precision=HIGH)
    same = (cum_reset[:, :, None] == cum_reset[:, None, :]) & (lower[None] > 0.5)
    spread = jnp.minimum(cum_log[:, :, :, None] - cum_log[:, :, None, :], 0.0)
    weight = jnp.where(same[None], jnp.exp(spread), 0.0)
    return (weight, cum_log, cum_reset)


def local(
    block_input,
    out_cotangent,
    segments,
    domain_tags,
    counts,
    attn_gain,
    mlp_gain,
    norm_gain,
    bound_table,
    w_input,
    w_forget,
    w_gate_mix,
    w_out,
    w_glu_gate,
    w_glu_up,
    w_glu_down,
):
    rows_dev, width = block_input.shape
    chans = w_input.shape[1]
    units = w_glu_gate.shape[1]
    seqs = segments.shape[0]
    total_rows = seqs * LEN
    nblk = LEN // BLK
    mp_index = lax.axis_index("mp")
    own_start = mp_index * rows_dev
    own_rows = block_input.astype(jnp.float32)
    own_inv1 = inverse_rms(own_rows)
    input_all = lax.all_gather(block_input, "mp", axis=0, tiled=True)
    input_all_f = input_all.astype(jnp.float32)
    normed_all = (input_all_f * inverse_rms(input_all_f) * attn_gain).astype(jnp.bfloat16)
    w_mix = jnp.concatenate([w_input, w_forget, w_gate_mix], axis=1)
    pre_mix = jnp.einsum("td,dc->ct", normed_all, w_mix, preferred_element_type=jnp.float32)
    pre_i = pre_mix[:chans].reshape(chans, seqs, LEN)
    pre_f = pre_mix[chans : 2 * chans].reshape(chans, seqs, LEN)
    pre_g = pre_mix[2 * chans :]
    shares = jax.nn.softmax(bound_table, axis=0)
    layer_ids = jnp.arange(NLAYER)
    pick = ((layer_ids >= 1) & (layer_ids <= LAYER)).astype(jnp.float32)[:, None]
    bound_vec = jnp.sum(shares * pick, axis=0)
    bound = bound_vec[:, None, None]
    sig_f = jax.nn.sigmoid(pre_f)
    forget = bound + (1.0 - bound) * sig_f
    act_i = jax.nn.silu(pre_i)
    update = act_i * (1.0 - forget)
    keep = jnp.concatenate(
        [
            jnp.zeros((seqs, 1), jnp.float32),
            (segments[:, 1:] == segments[:, :-1]).astype(jnp.float32),
        ],
        axis=1,
    )
    positions = jnp.arange(BLK)
    lower = (positions[None, :] <= positions[:, None]).astype(jnp.float32)

    def split_blocks(arr):
        arr = arr.reshape(arr.shape[:-1] + (nblk, BLK))
        return jnp.moveaxis(arr, -2, 0)

    def join_blocks(arr):
        arr = jnp.moveaxis(arr, 0, -2)
        return arr.reshape(arr.shape[:-2] + (LEN,))

    log_blocks = split_blocks(jnp.log(forget))
    reset_blocks = split_blocks(1.0 - keep)

    def forward_step(state, blk):
        log_blk, reset_blk, update_blk = blk
        weight, cum_log, cum_reset = block_terms(log_blk, reset_blk, lower)
        lead = jnp.where(cum_reset[None] == 0.0, jnp.exp(cum_log), 0.0)
        states_blk = (
            jnp.einsum("cstu,csu->cst", weight, update_blk, precision=HIGH)
            + lead * state[:, :, None]
        )
        return (states_blk[:, :, -1], states_blk)

    _, state_blocks = lax.scan(
        forward_step,
        jnp.zeros((chans, seqs), jnp.float32),
        (log_blocks, reset_blocks, split_blocks(update)),
    )
    states3 = join_blocks(state_blocks)
    states = states3.reshape(chans, total_rows)
    square_sum = lax.psum(jnp.sum(states * states, axis=0), "mp")
    rec_inv = lax.rsqrt(square_sum / width + EPS)
    unit_states = states * rec_inv[None, :]
    act_g = jax.nn.silu(pre_g)
    gated = (unit_states * norm_gain[:, None] * act_g).astype(jnp.bfloat16)
    partial_mix = jnp.einsum("ct,cd->td", gated, w_out, preferred_element_type=jnp.float32)
    middle_all = input_all_f + lax.psum(partial_mix.astype(jnp.bfloat16), "mp").astype(jnp.float32)
    normed_two_all = (middle_all * inverse_rms(middle_all) * mlp_gain).astype(jnp.bfloat16)
    middle = lax.dynamic_slice_in_dim(middle_all, own_start, rows_dev, 0)
    own_inv2 = inverse_rms(middle)
    w_glu = jnp.concatenate([w_glu_gate, w_glu_up], axis=1)
    gate_up = jnp.dot(normed_two_all, w_glu, preferred_element_type=jnp.float32)
    gate = gate_up[:, :units]
    up = gate_up[:, units:]
    act_gate = jax.nn.silu(gate)
    hidden = (act_gate * up).astype(jnp.bfloat16)
    piece = hidden
    final = middle + lax.psum_scatter(
        jnp.dot(piece, w_glu_down, preferred_element_type=jnp.float32).astype(jnp.bfloat16),
        "mp",
        scatter_dimension=0,
        tiled=True,
    ).astype(jnp.float32)
    result = final.astype(jnp.bfloat16)
    domain_hit = (domain_tags[:, None] == jnp.arange(NDOM)[None, :]).astype(jnp.float32)
    seq_count = jnp.dot(domain_hit, counts.astype(jnp.float32)[:, None], precision=HIGH)[:, 0]
    seq_weight = lax.rsqrt(seq_count)
    cot_all = lax.all_gather(out_cotangent, "mp", axis=0, tiled=True)
    grad_all = (
        cot_all.astype(jnp.float32).reshape(seqs, LEN, width) * seq_weight[:, None, None]
    ).reshape(total_rows, width)
    grad_all_b = grad_all.astype(jnp.bfloat16)
    grad_own = lax.dynamic_slice_in_dim(grad_all, own_start, rows_dev, 0)
    grad_hidden = jnp.einsum(
        "td,fd->tf", grad_all_b, w_glu_down, preferred_element_type=jnp.float32
    )
    down_term = jnp.einsum("tf,td->fd", hidden, grad_all_b, preferred_element_type=jnp.float32)
    grad_gate = grad_hidden * up * silu_slope(gate)
    grad_up = grad_hidden * act_gate
    grad_gate_up = jnp.concatenate([grad_gate, grad_up], axis=1).astype(jnp.bfloat16)
    piece = grad_gate_up
    grad_normed_two = lax.psum_scatter(
        jnp.einsum("tf,df->td", piece, w_glu, preferred_element_type=jnp.float32).astype(
            jnp.bfloat16
        ),
        "mp",
        scatter_dimension=0,
        tiled=True,
    ).astype(jnp.float32)
    back_two, mlp_gain_term = norm_back(grad_normed_two, middle, own_inv2, mlp_gain)
    grad_middle = grad_own + back_two
    middle_grad_all = lax.all_gather(grad_middle.astype(jnp.bfloat16), "mp", axis=0, tiled=True)
    grad_gated = jnp.einsum("td,cd->ct", middle_grad_all, w_out, preferred_element_type=jnp.float32)
    out_term = jnp.einsum("ct,td->cd", gated, middle_grad_all, preferred_element_type=jnp.float32)
    grad_unit = grad_gated * norm_gain[:, None] * act_g
    norm_gain_term = jnp.sum(grad_gated * unit_states * act_g, axis=1)
    grad_pre_g = grad_gated * unit_states * norm_gain[:, None] * silu_slope(pre_g)
    inner = lax.psum(jnp.sum(grad_unit * unit_states, axis=0), "mp")
    grad_states = rec_inv[None, :] * (grad_unit - unit_states * (inner / width)[None, :])
    forget_heads = split_blocks(forget)[..., 0]
    keep_heads = split_blocks(keep)[..., 0]

    def backward_step(carry, blk):
        log_blk, reset_blk, grad_blk, forget_head, keep_head = blk
        weight, cum_log, cum_reset = block_terms(log_blk, reset_blk, lower)
        trailing = jnp.where(
            (cum_reset == cum_reset[:, -1:])[None], jnp.exp(cum_log[:, :, -1:] - cum_log), 0.0
        )
        total = (
            jnp.einsum("cstu,cst->csu", weight, grad_blk, precision=HIGH)
            + trailing * carry[:, :, None]
        )
        return (forget_head * keep_head[None] * total[:, :, 0], total)

    _, grad_blocks = lax.scan(
        backward_step,
        jnp.zeros((chans, seqs), jnp.float32),
        (
            log_blocks,
            reset_blocks,
            split_blocks(grad_states.reshape(chans, seqs, LEN)),
            forget_heads,
            keep_heads,
        ),
        reverse=True,
    )
    grad_update = join_blocks(grad_blocks)
    prior = jnp.concatenate([jnp.zeros((chans, seqs, 1), jnp.float32), states3[:, :, :-1]], axis=2)
    grad_forget = grad_update * keep[None] * prior - grad_update * act_i
    grad_pre_i = grad_update * (1.0 - forget) * silu_slope(pre_i)
    grad_pre_f = grad_forget * (1.0 - bound) * sig_f * (1.0 - sig_f)
    bound_grad = jnp.sum(grad_forget * (1.0 - sig_f), axis=(1, 2))
    pick_grad = pick * bound_grad[None, :]
    table_term = shares * (pick_grad - jnp.sum(shares * pick_grad, axis=0, keepdims=True))
    grad_pre = jnp.concatenate(
        [grad_pre_i.reshape(chans, total_rows), grad_pre_f.reshape(chans, total_rows), grad_pre_g],
        axis=0,
    ).astype(jnp.bfloat16)
    piece = grad_pre
    grad_normed = lax.psum_scatter(
        jnp.einsum("ct,dc->td", piece, w_mix, preferred_element_type=jnp.float32).astype(
            jnp.bfloat16
        ),
        "mp",
        scatter_dimension=0,
        tiled=True,
    ).astype(jnp.float32)
    back_one, attn_gain_term = norm_back(grad_normed, own_rows, own_inv1, attn_gain)
    grad_block_input = grad_middle + back_one
    mix_part = jnp.einsum("tk,ct->kc", normed_all, grad_pre, preferred_element_type=jnp.float32)
    glu_part = jnp.einsum(
        "tk,tf->kf", normed_two_all, grad_gate_up, preferred_element_type=jnp.float32
    )
    weight_grads = lax.psum_scatter(
        jnp.concatenate([mix_part, glu_part], axis=1).astype(jnp.bfloat16),
        "dp",
        scatter_dimension=0,
        tiled=True,
    ).astype(jnp.float32)
    out_grad, down_grad = (
        lax.psum_scatter(
            out_term.astype(jnp.bfloat16), "dp", scatter_dimension=1, tiled=True
        ).astype(jnp.float32),
        lax.psum_scatter(
            down_term.astype(jnp.bfloat16), "dp", scatter_dimension=1, tiled=True
        ).astype(jnp.float32),
    )
    groups = lax.axis_size("mp")
    onehot = (jnp.arange(groups) == mp_index).astype(jnp.float32)
    norm_full = (onehot[:, None] * norm_gain_term[None, :]).reshape(width)
    table_full = (table_term[:, None, :] * onehot[None, :, None]).reshape(NLAYER, width)
    attn_sum, mlp_sum, norm_sum, table_sum = lax.psum(
        (attn_gain_term, mlp_gain_term, norm_full, table_full), ("dp", "mp")
    )
    grad_input = weight_grads[:, :chans]
    grad_forget_w = weight_grads[:, chans : 2 * chans]
    grad_gate_mix = weight_grads[:, 2 * chans : 3 * chans]
    grad_glu_gate = weight_grads[:, 3 * chans : 3 * chans + units]
    grad_glu_up = weight_grads[:, 3 * chans + units :]
    return (
        result,
        grad_block_input,
        attn_sum,
        mlp_sum,
        norm_sum,
        table_sum,
        grad_input,
        grad_forget_w,
        grad_gate_mix,
        out_grad,
        grad_glu_gate,
        grad_glu_up,
        down_grad,
    )


def solution(mesh):
    placed = (
        P(("dp", "mp"), None),
        P(("dp", "mp"), None),
        P("dp", None),
        P("dp"),
        P(),
        P(),
        P(),
        P("mp"),
        P(None, "mp"),
        P(None, "mp"),
        P(None, "mp"),
        P(None, "mp"),
        P("mp", None),
        P(None, "mp"),
        P(None, "mp"),
        P("mp", None),
    )
    return jax.shard_map(
        local,
        mesh=mesh,
        in_specs=placed,
        out_specs=(
            P(("dp", "mp"), None),
            P(("dp", "mp"), None),
            P(),
            P(),
            P(),
            P(),
            P("dp", "mp"),
            P("dp", "mp"),
            P("dp", "mp"),
            P("mp", "dp"),
            P("dp", "mp"),
            P("dp", "mp"),
            P("mp", "dp"),
        ),
        check_vma=False,
    )
```

profile of v0, /device:TPU:10, one launch (start us, length us, event | category | flops | bytes accessed | tf_op | source)
XLA Modules:
  0.0 1434.1 jit_solution(5197083218827090929)
XLA Ops:
  17.3 66.8 %all-gather.4.cloned.1.call-done = bf16[1024,2048]{1,0:T(8,128)(2,1)} async-done(((bf16[128,2048]{1,0:T(8,128)(2,1)}), bf16[1024,2048]{1,0:T(8,128)(2,1)}) %all-gather.4.cloned.1.call-update) | async-done | bytes 4194320 | tf_op jit(solution)/shard_map/all_gather | solution.py:68
  100.1 259.9 %while.32 = (s32[]{:T(128)}, f32[256,1]{0,1:T(1,128)S(1)}, f32[8,256,1,128]{1,3,2,0:T(8,128)}, f32[8,1,128]{2,1,0:T(1,128)S(1)}, f32[8,256,1,128]{3,2,1,0:T(1,128)}, /*index=5*/f32[8,256,1,128]{3,2,1,0:T(1,128)}, s32[]{:T(128)}) while((s32[]{:T(128)}, f32[256,1]{0,1:T(1,128)S(1)}, f32[8,256,1,128]{1,3,2,0:T(8,128)}, ...), condition=%wide.region_5.6_spmd.clone.clone, body=%wide.region_4.0_spmd.clone.clone.sunk | while | flops 113787008 | bytes 2398181 | solution.py:116
  102.0 28.5 %fusion.137 = f32[256,1,128]{2,1,0:T(1,128)S(1)} fusion(f32[256,128]{1,0:T(8,128)S(1)} %copy.93, pred[128,128]{1,0:T(8,128)(4,1)S(1)} %fusion.136, f32[8,256,1,128]{3,2,1,0:T(1,128)} %get-tuple-element.526, s32[]{:T(128)S(6)} %copy.104), kind=kOutput, calls=%fused_computation.2.clone.1 | convolution fusion | flops 62914560 | bytes 540676 | tf_op jit(solution)/shard_map/while/body/eval_jaxpr/cstu,csu->cst/dot_general | solution.py:111
  133.1 28.5 %fusion.137 = f32[256,1,128]{2,1,0:T(1,128)S(1)} fusion(f32[256,128]{1,0:T(8,128)S(1)} %copy.93, pred[128,128]{1,0:T(8,128)(4,1)S(1)} %fusion.136, f32[8,256,1,128]{3,2,1,0:T(1,128)} %get-tuple-element.526, s32[]{:T(128)S(6)} %copy.104), kind=kOutput, calls=%fused_computation.2.clone.1 | convolution fusion | flops 62914560 | bytes 540676 | tf_op jit(solution)/shard_map/while/body/eval_jaxpr/cstu,csu->cst/dot_general | solution.py:111
  164.3 28.5 %fusion.137 = f32[256,1,128]{2,1,0:T(1,128)S(1)} fusion(f32[256,128]{1,0:T(8,128)S(1)} %copy.93, pred[128,128]{1,0:T(8,128)(4,1)S(1)} %fusion.136, f32[8,256,1,128]{3,2,1,0:T(1,128)} %get-tuple-element.526, s32[]{:T(128)S(6)} %copy.104), kind=kOutput, calls=%fused_computation.2.clone.1 | convolution fusion | flops 62914560 | bytes 540676 | tf_op jit(solution)/shard_map/while/body/eval_jaxpr/cstu,csu->cst/dot_general | solution.py:111
  195.4 28.5 %fusion.137 = f32[256,1,128]{2,1,0:T(1,128)S(1)} fusion(f32[256,128]{1,0:T(8,128)S(1)} %copy.93, pred[128,128]{1,0:T(8,128)(4,1)S(1)} %fusion.136, f32[8,256,1,128]{3,2,1,0:T(1,128)} %get-tuple-element.526, s32[]{:T(128)S(6)} %copy.104), kind=kOutput, calls=%fused_computation.2.clone.1 | convolution fusion | flops 62914560 | bytes 540676 | tf_op jit(solution)/shard_map/while/body/eval_jaxpr/cstu,csu->cst/dot_general | solution.py:111
  226.6 28.5 %fusion.137 = f32[256,1,128]{2,1,0:T(1,128)S(1)} fusion(f32[256,128]{1,0:T(8,128)S(1)} %copy.93, pred[128,128]{1,0:T(8,128)(4,1)S(1)} %fusion.136, f32[8,256,1,128]{3,2,1,0:T(1,128)} %get-tuple-element.526, s32[]{:T(128)S(6)} %copy.104), kind=kOutput, calls=%fused_computation.2.clone.1 | convolution fusion | flops 62914560 | bytes 540676 | tf_op jit(solution)/shard_map/while/body/eval_jaxpr/cstu,csu->cst/dot_general | solution.py:111
  257.7 28.5 %fusion.137 = f32[256,1,128]{2,1,0:T(1,128)S(1)} fusion(f32[256,128]{1,0:T(8,128)S(1)} %copy.93, pred[128,128]{1,0:T(8,128)(4,1)S(1)} %fusion.136, f32[8,256,1,128]{3,2,1,0:T(1,128)} %get-tuple-element.526, s32[]{:T(128)S(6)} %copy.104), kind=kOutput, calls=%fused_computation.2.clone.1 | convolution fusion | flops 62914560 | bytes 540676 | tf_op jit(solution)/shard_map/while/body/eval_jaxpr/cstu,csu->cst/dot_general | solution.py:111
  288.9 28.5 %fusion.137 = f32[256,1,128]{2,1,0:T(1,128)S(1)} fusion(f32[256,128]{1,0:T(8,128)S(1)} %copy.93, pred[128,128]{1,0:T(8,128)(4,1)S(1)} %fusion.136, f32[8,256,1,128]{3,2,1,0:T(1,128)} %get-tuple-element.526, s32[]{:T(128)S(6)} %copy.104), kind=kOutput, calls=%fused_computation.2.clone.1 | convolution fusion | flops 62914560 | bytes 540676 | tf_op jit(solution)/shard_map/while/body/eval_jaxpr/cstu,csu->cst/dot_general | solution.py:111
  320.0 28.5 %fusion.137 = f32[256,1,128]{2,1,0:T(1,128)S(1)} fusion(f32[256,128]{1,0:T(8,128)S(1)} %copy.93, pred[128,128]{1,0:T(8,128)(4,1)S(1)} %fusion.136, f32[8,256,1,128]{3,2,1,0:T(1,128)} %get-tuple-element.526, s32[]{:T(128)S(6)} %copy.104), kind=kOutput, calls=%fused_computation.2.clone.1 | convolution fusion | flops 62914560 | bytes 540676 | tf_op jit(solution)/shard_map/while/body/eval_jaxpr/cstu,csu->cst/dot_general | solution.py:111
  364.0 16.6 %psum.49 = f32[1024]{0:T(1024)S(1)} all-reduce(f32[1024]{0:T(1024)S(1)} %bitcast.246), channel_id=1, replica_groups=mesh['dp'=4,'mp'=8] {'mp'}, use_global_device_ids=true, to_apply=%region_7.8 | all-reduce | flops 1024 | bytes 8192 | tf_op jit(solution)/shard_map/psum | solution.py:123
  395.8 145.9 %all-reduce.5.cloned.1.call-done = bf16[1024,2048]{1,0:T(8,128)(2,1)} async-done(((bf16[1024,2048]{1,0:T(8,128)(2,1)}), bf16[1024,2048]{1,0:T(8,128)(2,1)}) %all-reduce.5.cloned.1.call-update) | async-done | bytes 4194320 | tf_op jit(solution)/shard_map/psum | solution.py:129
  549.9 11.4 fusion.92
  561.3 56.1 %all-gather.6.cloned.1.call-done = bf16[1024,2048]{1,0:T(8,128)(2,1)} async-done(((bf16[128,2048]{1,0:T(8,128)(2,1)}), bf16[1024,2048]{1,0:T(8,128)(2,1)}) %all-gather.6.cloned.1.call-update) | async-done | bytes 4194320 | tf_op jit(solution)/shard_map/all_gather | solution.py:150
  647.5 79.2 %reduce-scatter.9.cloned.1.call-done = bf16[128,2048]{1,0:T(8,128)(2,1)} async-done(((bf16[1024,2048]{1,0:T(8,128)(2,1)}), bf16[128,2048]{1,0:T(8,128)(2,1)}) %reduce-scatter.9.cloned.1.call-update) | async-done | bytes 524304 | tf_op jit(solution)/shard_map/reduce_scatter | solution.py:164
  747.4 56.4 %all-gather.8.cloned.1.call-done = bf16[1024,2048]{1,0:T(8,128)(2,1)} async-done(((bf16[128,2048]{1,0:T(8,128)(2,1)}), bf16[1024,2048]{1,0:T(8,128)(2,1)}) %all-gather.8.cloned.1.call-update) | async-done | bytes 4194320 | tf_op jit(solution)/shard_map/all_gather | solution.py:174
  809.4 16.6 %psum.51 = f32[1024]{0:T(1024)S(1)} all-reduce(f32[1024]{0:T(1024)S(1)} %get-tuple-element.357), channel_id=1, replica_groups=mesh['dp'=4,'mp'=8] {'mp'}, use_global_device_ids=true, to_apply=%region_16.17 | all-reduce | flops 1024 | bytes 8192 | tf_op jit(solution)/shard_map/psum | solution.py:180
  835.1 182.9 %while.33 = (s32[]{:T(128)}, f32[256,1]{0,1:T(1,128)S(1)}, f32[8,256,1,128]{1,3,2,0:T(8,128)}, f32[8,256,1]{1,2,0:T(1,128)S(1)}, f32[8,1]{0,1:T(1,128)S(1)}, /*i...) while((s32[]{:T(128)}, f32[256,1]{0,1:T(1,128)S(1)}, ...), condition=%wide.region_18.19_spmd.clone.clone, body=%wide.region_17.18_spmd.clone.clone.sunk | while | flops 113853312 | bytes 2405947 | solution.py:197
  838.1 17.7 %fusion.148 = f32[256,1,128]{2,1,0:T(1,128)S(1)} fusion(f32[256,128]{1,0:T(8,128)S(1)} %copy.95, pred[128,128]{1,0:T(8,128)(4,1)S(1)} %fusion.147, f32[8,256,1,128]{3,2,1,0:T(1,128)} %get-tuple-element.557, s32[]{:T(128)S(6)} %sub.280), kind=kOutput, calls=%fused_computation.30.clone.1 | convolution fusion | flops 62914560 | bytes 540676 | tf_op jit(solution)/shard_map/while/body/eval_jaxpr/cstu,cst->csu/dot_general | solution.py:192
  861.0 17.7 %fusion.148 = f32[256,1,128]{2,1,0:T(1,128)S(1)} fusion(f32[256,128]{1,0:T(8,128)S(1)} %copy.95, pred[128,128]{1,0:T(8,128)(4,1)S(1)} %fusion.147, f32[8,256,1,128]{3,2,1,0:T(1,128)} %get-tuple-element.557, s32[]{:T(128)S(6)} %sub.280), kind=kOutput, calls=%fused_computation.30.clone.1 | convolution fusion | flops 62914560 | bytes 540676 | tf_op jit(solution)/shard_map/while/body/eval_jaxpr/cstu,cst->csu/dot_general | solution.py:192
  883.8 17.7 %fusion.148 = f32[256,1,128]{2,1,0:T(1,128)S(1)} fusion(f32[256,128]{1,0:T(8,128)S(1)} %copy.95, pred[128,128]{1,0:T(8,128)(4,1)S(1)} %fusion.147, f32[8,256,1,128]{3,2,1,0:T(1,128)} %get-tuple-element.557, s32[]{:T(128)S(6)} %sub.280), kind=kOutput, calls=%fused_computation.30.clone.1 | convolution fusion | flops 62914560 | bytes 540676 | tf_op jit(solution)/shard_map/while/body/eval_jaxpr/cstu,cst->csu/dot_general | solution.py:192
  906.6 17.7 %fusion.148 = f32[256,1,128]{2,1,0:T(1,128)S(1)} fusion(f32[256,128]{1,0:T(8,128)S(1)} %copy.95, pred[128,128]{1,0:T(8,128)(4,1)S(1)} %fusion.147, f32[8,256,1,128]{3,2,1,0:T(1,128)} %get-tuple-element.557, s32[]{:T(128)S(6)} %sub.280), kind=kOutput, calls=%fused_computation.30.clone.1 | convolution fusion | flops 62914560 | bytes 540676 | tf_op jit(solution)/shard_map/while/body/eval_jaxpr/cstu,cst->csu/dot_general | solution.py:192
  929.4 17.7 %fusion.148 = f32[256,1,128]{2,1,0:T(1,128)S(1)} fusion(f32[256,128]{1,0:T(8,128)S(1)} %copy.95, pred[128,128]{1,0:T(8,128)(4,1)S(1)} %fusion.147, f32[8,256,1,128]{3,2,1,0:T(1,128)} %get-tuple-element.557, s32[]{:T(128)S(6)} %sub.280), kind=kOutput, calls=%fused_computation.30.clone.1 | convolution fusion | flops 62914560 | bytes 540676 | tf_op jit(solution)/shard_map/while/body/eval_jaxpr/cstu,cst->csu/dot_general | solution.py:192
  952.3 17.7 %fusion.148 = f32[256,1,128]{2,1,0:T(1,128)S(1)} fusion(f32[256,128]{1,0:T(8,128)S(1)} %copy.95, pred[128,128]{1,0:T(8,128)(4,1)S(1)} %fusion.147, f32[8,256,1,128]{3,2,1,0:T(1,128)} %get-tuple-element.557, s32[]{:T(128)S(6)} %sub.280), kind=kOutput, calls=%fused_computation.30.clone.1 | convolution fusion | flops 62914560 | bytes 540676 | tf_op jit(solution)/shard_map/while/body/eval_jaxpr/cstu,cst->csu/dot_general | solution.py:192
  975.1 17.7 %fusion.148 = f32[256,1,128]{2,1,0:T(1,128)S(1)} fusion(f32[256,128]{1,0:T(8,128)S(1)} %copy.95, pred[128,128]{1,0:T(8,128)(4,1)S(1)} %fusion.147, f32[8,256,1,128]{3,2,1,0:T(1,128)} %get-tuple-element.557, s32[]{:T(128)S(6)} %sub.280), kind=kOutput, calls=%fused_computation.30.clone.1 | convolution fusion | flops 62914560 | bytes 540676 | tf_op jit(solution)/shard_map/while/body/eval_jaxpr/cstu,cst->csu/dot_general | solution.py:192
  997.9 17.7 %fusion.148 = f32[256,1,128]{2,1,0:T(1,128)S(1)} fusion(f32[256,128]{1,0:T(8,128)S(1)} %copy.95, pred[128,128]{1,0:T(8,128)(4,1)S(1)} %fusion.147, f32[8,256,1,128]{3,2,1,0:T(1,128)} %get-tuple-element.557, s32[]{:T(128)S(6)} %sub.280), kind=kOutput, calls=%fused_computation.30.clone.1 | convolution fusion | flops 62914560 | bytes 540676 | tf_op jit(solution)/shard_map/while/body/eval_jaxpr/cstu,cst->csu/dot_general | solution.py:192
  1042.2 13.5 convolution_convert_fusion
  1077.6 46.3 %reduce-scatter.11.cloned.1.call-done = bf16[128,2048]{1,0:T(8,128)(2,1)} async-done(((bf16[1024,2048]{1,0:T(8,128)(2,1)}), bf16[128,2048]{1,0:T(8,128)(2,1)}) %reduce-scatter.11.cloned.1.call-update) | async-done | bytes 524304 | tf_op jit(solution)/shard_map/reduce_scatter | solution.py:222
  1125.4 42.5 %all-reduce.1 = (f32[2048]{0:T(1024)}, f32[2048]{0:T(1024)}, f32[2048]{0:T(1024)}) all-reduce(f32[2048]{0:T(1024)S(1)} %get-tuple-element.358, f32[2048]{0:T(1024)S(1)} %get-tuple-element.354, f32[2048]{0:T(1024)S(1)} %mul.516), channel_id=1, replica_groups=mesh['dp'=4,'mp'=8] {'dp','mp'}, use_global_device_ids=true, to_apply=%region_22.23 | all-reduce | flops 6144 | bytes 49152 | tf_op jit(solution)/shard_map/psum | solution.py:254
  1167.8 48.6 %reduce-scatter.7.cloned.1.call-done = bf16[128,2048]{1,0:T(8,128)(2,1)} async-done(((bf16[1024,2048]{1,0:T(8,128)(2,1)}), bf16[128,2048]{1,0:T(8,128)(2,1)}) %reduce-scatter.7.cloned.1.call-update) | async-done | bytes 524304 | tf_op jit(solution)/shard_map/reduce_scatter | solution.py:140
  1220.1 72.7 %reduce-scatter.13.cloned.1.call-done = bf16[512,2176]{0,1:T(8,128)(2,1)} async-done(((bf16[2048,2176]{0,1:T(8,128)(2,1)}), bf16[512,2176]{0,1:T(8,128)(2,1)}) %reduce-scatter.13.cloned.1.call-update) | async-done | bytes 2228240 | tf_op jit(solution)/shard_map/reduce_scatter | solution.py:236
  1302.5 123.1 %all-reduce.7.cloned.1.call-done = f32[24,2048]{1,0:T(8,128)} async-done(((f32[24,2048]{1,0:T(8,128)}), f32[24,2048]{1,0:T(8,128)}) %all-reduce.7.cloned.1.call-update) | async-done | bytes 196624 | tf_op jit(solution)/shard_map/psum | solution.py:254
  (366 shorter events, 240.0 us)
Async XLA Ops:
  7.2 610.2 %copy-start = (bf16[704,2048]{1,0:T(8,128)(2,1)S(1)}, bf16[704,2048]{1,0:T(8,128)(2,1)}, u32[]{:S(2)}) copy-start(bf16[704,2048]{1,0:T(8,128)(2,1)} %param.35) | copy-start | bytes 8650756
  7.2 76.9 %all-gather.4.cloned.1.call-start = ((), (), s32[]{:S(2)}) async-start(), calls=%async_computation.6 | async-start | bytes 4718592 | tf_op jit(solution)/shard_map/all_gather | solution.py:68
  7.9 533.8 %all-reduce.5.cloned.1.call-start = ((), (), s32[]{:S(2)}) async-start(), calls=%async_computation.7 | async-start | bytes 8388608 | tf_op jit(solution)/shard_map/psum | solution.py:129
  8.8 7.4 copy-start.11
  11.4 81.7 %copy-start.24 = (f32[256]{0:T(256)}, f32[256]{0:T(256)S(1)}, u32[]{:S(2)}) copy-start(f32[256]{0:T(256)S(1)} %multiply_reduce_fusion.4) | copy-start | bytes 3076
  11.4 81.7 %copy-start.22 = (f32[256]{0:T(256)}, f32[256]{0:T(256)S(1)}, u32[]{:S(2)}) copy-start(f32[256]{0:T(256)S(1)} %broadcast_subtract_fusion.1) | copy-start | bytes 3076
  13.8 73.5 %copy-start.18 = (f32[2048]{0:T(1024)S(1)}, f32[2048]{0:T(1024)}, u32[]{:S(2)}) copy-start(f32[2048]{0:T(1024)} %param.25) | copy-start | bytes 24580
  87.5 5.6 copy-start.30
  100.1 280.5 %copy-start.32 = (f32[256]{0:T(256)S(1)}, f32[256]{0:T(256)}, u32[]{:S(2)}) copy-start(f32[256]{0:T(256)} %param.27) | copy-start | bytes 3076
  387.1 230.3 %all-gather.6.cloned.1.call-start = ((), (), s32[]{:S(2)}) async-start(), calls=%async_computation.9 | async-start | bytes 4718592 | tf_op jit(solution)/shard_map/all_gather | solution.py:150
  387.8 338.9 %reduce-scatter.9.cloned.1.call-start = ((), (), s32[]{:S(2)}) async-start(), calls=%async_computation.10 | async-start | bytes 4718592 | tf_op jit(solution)/shard_map/reduce_scatter | solution.py:164
  389.8 4.2 copy-start.10
  395.8 154.1 %copy-start.17 = (f32[2048]{0:T(1024)S(1)}, f32[2048]{0:T(1024)}, u32[]{:S(2)}) copy-start(f32[2048]{0:T(1024)} %param.26) | copy-start | bytes 24580
  541.7 8.2 copy-start.4
  541.7 8.2 copy-start.9
  639.4 164.4 %all-gather.8.cloned.1.call-start = ((), (), s32[]{:S(2)}) async-start(), calls=%async_computation.11 | async-start | bytes 4718592 | tf_op jit(solution)/shard_map/all_gather | solution.py:174
  731.4 340.9 %reduce-scatter.17.cloned.1.call-start = ((), (), s32[]{:S(2)}) async-start(), calls=%async_computation.16 | async-start | bytes 3604480 | tf_op jit(solution)/shard_map/reduce_scatter | solution.py:246
  739.3 336.5 %reduce-scatter.15.cloned.1.call-start = ((), (), s32[]{:S(2)}) async-start(), calls=%async_computation.15 | async-start | bytes 1310720 | tf_op jit(solution)/shard_map/reduce_scatter | solution.py:243
  826.0 5.7 copy-start.33
  834.0 289.9 %reduce-scatter.11.cloned.1.call-start = ((), (), s32[]{:S(2)}) async-start(), calls=%async_computation.12 | async-start | bytes 4718592 | tf_op jit(solution)/shard_map/reduce_scatter | solution.py:222
  1020.6 6.0 copy-start.23
  1023.1 3.8 copy-start.6
  1023.1 3.9 copy-start.25
  1035.5 180.9 %reduce-scatter.7.cloned.1.call-start = ((), (), s32[]{:S(2)}) async-start(), calls=%async_computation.8 | async-start | bytes 4718592 | tf_op jit(solution)/shard_map/reduce_scatter | solution.py:140
  1042.0 13.6 copy-start.19
  1042.1 13.6 copy-start.31
  1042.1 250.7 %reduce-scatter.13.cloned.1.call-start = ((), (), s32[]{:S(2)}) async-start(), calls=%async_computation.14 | async-start | bytes 11141120 | tf_op jit(solution)/shard_map/reduce_scatter | solution.py:236
  1042.1 13.6 copy-start.5
  1042.1 13.6 copy-start.14
  1042.1 13.6 copy-start.16
  1071.0 3.7 copy-start.29
  1071.1 354.5 %all-reduce.7.cloned.1.call-start = ((), (), s32[]{:S(2)}) async-start(), calls=%async_computation.13 | async-start | bytes 393216 | tf_op jit(solution)/shard_map/psum | solution.py:254
  (16 other events, 37.3 us)
Sparse Core Ops, SparseCore 0:
  10.2 73.8 all-gather.3
  387.2 154.4 all-reduce.4
  543.8 73.4 all-gather.5
  639.5 87.1 reduce-scatter.8
  731.5 72.2 all-gather.7
  806.3 34.3 reduce-scatter.16
  843.2 24.8 reduce-scatter.14
  1035.7 88.1 reduce-scatter.10
  1127.5 88.8 reduce-scatter.6
  1219.0 73.6 reduce-scatter.12
  1299.8 125.7 all-reduce.6
where the time goes:
time: 1440 us; the launch traced here: 1430 us
  waiting for transfers between devices  697 us (48%)
  matrix products  468 us (32%)
  other arithmetic  86.1 us (6%)
  local copies, waits for them, and re-layouts  78.9 us (5%)
  blocking collectives  75.7 us (5%)
  between operations  16.1 us (1%)
    dot_general x8, matrix products, forward_step(): jnp.einsum('cstu,csu->cst', weight, update_blk, precision=HIGH)  228 us
    psum x1, waiting for transfers between devices, local(): lax.psum(partial_mix.astype(jnp.bfloat16), 'mp').astype(jnp.float32)  146 us
    dot_general x8, matrix products, backward_step(): jnp.einsum('cstu,cst->csu', weight, grad_blk, precision=HIGH)  142 us
    psum x1, waiting for transfers between devices, local(): lax.psum((attn_gain_term, mlp_gain_term, norm_full, table_full), ('dp', '...  123 us
    reduce_scatter x1, waiting for transfers between devices, local(): lax.psum_scatter(jnp.einsum('tf,df->td', piece, w_glu, preferred_element_...  79.2 us
    reduce_scatter x1, waiting for transfers between devices, local(): lax.psum_scatter(jnp.concatenate([mix_part, glu_part], axis=1).astype(jnp...  72.7 us
    all_gather x1, waiting for transfers between devices, local(): input_all = lax.all_gather(block_input, 'mp', axis=0, tiled=True)  66.8 us
    all_gather x1, waiting for transfers between devices, local(): lax.all_gather(grad_middle.astype(jnp.bfloat16), 'mp', axis=0, tiled=True)  56.4 us
  transfers between devices with their start and end apart: 11, of which 9 were waited for; matrix products, arithmetic and copies ran while one was open for 23% of the time, Pallas kernels for 0%

commit v1 on v0

--- a/solution.py
+++ b/solution.py
@@ -147,7 +147,12 @@
     domain_hit = (domain_tags[:, None] == jnp.arange(NDOM)[None, :]).astype(jnp.float32)
     seq_count = jnp.dot(domain_hit, counts.astype(jnp.float32)[:, None], precision=HIGH)[:, 0]
     seq_weight = lax.rsqrt(seq_count)
-    cot_all = lax.all_gather(out_cotangent, "mp", axis=0, tiled=True)
+    ring = [out_cotangent]
+    for hop in range(7):
+        ring.append(lax.ppermute(ring[-1], "mp", [(dev, (dev + 1) % 8) for dev in range(8)]))
+    cot_all = jnp.roll(
+        jnp.concatenate(ring[::-1], axis=0), (lax.axis_index("mp") + 1) * ring[0].shape[0], axis=0
+    )
     grad_all = (
         cot_all.astype(jnp.float32).reshape(seqs, LEN, width) * seq_weight[:, None, None]
     ).reshape(total_rows, width)

time: 1440 us -> 1430 us (level)
  waiting for transfers between devices: 697 us -> 644 us
  starting transfers between devices: 0.85 us -> 30.3 us
  local copies, waits for them, and re-layouts: 78.9 us -> 101 us
    ppermute x0 -> x7, waiting for transfers between devices: none -> 87.9 us  [local(): lax.ppermute(ring[-1], 'mp', [(dev, (dev + 1) % 8) for dev in range(8)])]
    all_gather x1, waiting for transfers between devices: 66.8 us -> 0.01 us  [local(): input_all = lax.all_gather(block_input, 'mp', axis=0, tiled=True)]
    all_gather x1 -> x0, waiting for transfers between devices: 56.1 us -> none  [local(): cot_all = lax.all_gather(out_cotangent, 'mp', axis=0, tiled=True)]
    ppermute x0 -> x7, starting transfers between devices: none -> 29.5 us  [local(): lax.ppermute(ring[-1], 'mp', [(dev, (dev + 1) % 8) for dev in range(8)])]
    unnamed x91 -> x126, local copies, waits for them, and re-layouts: 25 us -> 45.6 us
    psum x1, waiting for transfers between devices: 146 us -> 127 us  [local(): lax.psum(partial_mix.astype(jnp.bfloat16), 'mp').astype(jnp.float32)]
  transfers between devices with their start and end apart: 11 -> 17, of which waited for: 9 -> 13; matrix products, arithmetic and copies ran while one was open for 23% -> 42% of each run, Pallas kernels for 0% -> 0%
where the time goes in v1:
time: 1430 us; the launch traced here: 1420 us
  waiting for transfers between devices  644 us (45%)
  matrix products  460 us (32%)
  local copies, waits for them, and re-layouts  101 us (7%)
  other arithmetic  86.2 us (6%)
  blocking collectives  79 us (6%)
  starting transfers between devices  30.3 us (2%)
  between operations  16.5 us (1%)
    dot_general x8, matrix products, forward_step(): jnp.einsum('cstu,csu->cst', weight, update_blk, precision=HIGH)  228 us
    dot_general x8, matrix products, backward_step(): jnp.einsum('cstu,cst->csu', weight, grad_blk, precision=HIGH)  142 us
    psum x1, waiting for transfers between devices, local(): lax.psum(partial_mix.astype(jnp.bfloat16), 'mp').astype(jnp.float32)  127 us
    psum x1, waiting for transfers between devices, local(): lax.psum((attn_gain_term, mlp_gain_term, norm_full, table_full), ('dp', '...  123 us
    ppermute x7, waiting for transfers between devices, local(): lax.ppermute(ring[-1], 'mp', [(dev, (dev + 1) % 8) for dev in range(8)])  87.9 us
    reduce_scatter x1, waiting for transfers between devices, local(): lax.psum_scatter(jnp.einsum('tf,df->td', piece, w_glu, preferred_element_...  81 us
    reduce_scatter x1, waiting for transfers between devices, local(): lax.psum_scatter(jnp.concatenate([mix_part, glu_part], axis=1).astype(jnp...  72.9 us
    all_gather x1, waiting for transfers between devices, local(): lax.all_gather(grad_middle.astype(jnp.bfloat16), 'mp', axis=0, tiled=True)  56.4 us
  transfers between devices with their start and end apart: 17, of which 13 were waited for; matrix products, arithmetic and copies ran while one was open for 42% of the time, Pallas kernels for 0%

profile of v1, /device:TPU:10, one launch (start us, length us, event | category | flops | bytes accessed | tf_op | source)
XLA Modules:
  0.0 1419.4 jit_solution(4213988494896739398)
XLA Ops:
  9.5 14.0 collective-permute-done
  25.6 24.7 %collective-permute-done.1 = bf16[128,2048]{1,0:T(8,128)(2,1)S(1)} collective-permute-done((bf16[128,2048]{1,0:T(8,128)(2,1)S(1)}, bf16[128,2048]{1,0:T(8,128)(2,1)S(1)}, u32[]{:S(2)}, u32[]{:S(2)}) %collective-permute-start.1) | collective-permute-done | bytes 524320 | tf_op jit(solution)/shard_map/ppermute | solution.py:152
  52.2 18.4 %collective-permute-done.2 = bf16[128,2048]{1,0:T(8,128)(2,1)} collective-permute-done((bf16[128,2048]{1,0:T(8,128)(2,1)S(1)}, bf16[128,2048]{1,0:T(8,128)(2,1)}, u32[]{:S(2)}, u32[]{:S(2)}) %collective-permute-start.2) | collective-permute-done | bytes 524320 | tf_op jit(solution)/shard_map/ppermute | solution.py:152
  82.7 14.0 collective-permute-done.3
  153.5 249.9 %while.32 = (s32[]{:T(128)}, f32[256,1]{0,1:T(1,128)S(1)}, f32[8,256,1,128]{1,3,2,0:T(8,128)}, f32[8,1,128]{2,1,0:T(1,128)S(1)}, f32[8,256,1,128]{3,2,1,0:T(1,128)}, /*index=5*/f32[8,256,1,128]{3,2,1,0:T(1,128)}, s32[]{:T(128)}) while((s32[]{:T(128)}, f32[256,1]{0,1:T(1,128)S(1)}, f32[8,256,1,128]{1,3,2,0:T(8,128)}, ...), condition=%wide.region_5.6_spmd.clone.clone, body=%wide.region_4.0_spmd.clone.clone.sunk | while | flops 113787008 | bytes 2398181 | solution.py:116
  155.4 28.5 %fusion.139 = f32[256,1,128]{2,1,0:T(1,128)S(1)} fusion(f32[256,128]{1,0:T(8,128)S(1)} %copy.93, pred[128,128]{1,0:T(8,128)(4,1)S(1)} %fusion.138, f32[8,256,1,128]{3,2,1,0:T(1,128)} %get-tuple-element.526, s32[]{:T(128)S(6)} %copy.104), kind=kOutput, calls=%fused_computation.2.clone.1 | convolution fusion | flops 62914560 | bytes 540676 | tf_op jit(solution)/shard_map/while/body/eval_jaxpr/cstu,csu->cst/dot_general | solution.py:111
  186.5 28.5 %fusion.139 = f32[256,1,128]{2,1,0:T(1,128)S(1)} fusion(f32[256,128]{1,0:T(8,128)S(1)} %copy.93, pred[128,128]{1,0:T(8,128)(4,1)S(1)} %fusion.138, f32[8,256,1,128]{3,2,1,0:T(1,128)} %get-tuple-element.526, s32[]{:T(128)S(6)} %copy.104), kind=kOutput, calls=%fused_computation.2.clone.1 | convolution fusion | flops 62914560 | bytes 540676 | tf_op jit(solution)/shard_map/while/body/eval_jaxpr/cstu,csu->cst/dot_general | solution.py:111
  217.7 28.5 %fusion.139 = f32[256,1,128]{2,1,0:T(1,128)S(1)} fusion(f32[256,128]{1,0:T(8,128)S(1)} %copy.93, pred[128,128]{1,0:T(8,128)(4,1)S(1)} %fusion.138, f32[8,256,1,128]{3,2,1,0:T(1,128)} %get-tuple-element.526, s32[]{:T(128)S(6)} %copy.104), kind=kOutput, calls=%fused_computation.2.clone.1 | convolution fusion | flops 62914560 | bytes 540676 | tf_op jit(solution)/shard_map/while/body/eval_jaxpr/cstu,csu->cst/dot_general | solution.py:111
  248.8 28.5 %fusion.139 = f32[256,1,128]{2,1,0:T(1,128)S(1)} fusion(f32[256,128]{1,0:T(8,128)S(1)} %copy.93, pred[128,128]{1,0:T(8,128)(4,1)S(1)} %fusion.138, f32[8,256,1,128]{3,2,1,0:T(1,128)} %get-tuple-element.526, s32[]{:T(128)S(6)} %copy.104), kind=kOutput, calls=%fused_computation.2.clone.1 | convolution fusion | flops 62914560 | bytes 540676 | tf_op jit(solution)/shard_map/while/body/eval_jaxpr/cstu,csu->cst/dot_general | solution.py:111
  280.0 28.5 %fusion.139 = f32[256,1,128]{2,1,0:T(1,128)S(1)} fusion(f32[256,128]{1,0:T(8,128)S(1)} %copy.93, pred[128,128]{1,0:T(8,128)(4,1)S(1)} %fusion.138, f32[8,256,1,128]{3,2,1,0:T(1,128)} %get-tuple-element.526, s32[]{:T(128)S(6)} %copy.104), kind=kOutput, calls=%fused_computation.2.clone.1 | convolution fusion | flops 62914560 | bytes 540676 | tf_op jit(solution)/shard_map/while/body/eval_jaxpr/cstu,csu->cst/dot_general | solution.py:111
  311.1 28.5 %fusion.139 = f32[256,1,128]{2,1,0:T(1,128)S(1)} fusion(f32[256,128]{1,0:T(8,128)S(1)} %copy.93, pred[128,128]{1,0:T(8,128)(4,1)S(1)} %fusion.138, f32[8,256,1,128]{3,2,1,0:T(1,128)} %get-tuple-element.526, s32[]{:T(128)S(6)} %copy.104), kind=kOutput, calls=%fused_computation.2.clone.1 | convolution fusion | flops 62914560 | bytes 540676 | tf_op jit(solution)/shard_map/while/body/eval_jaxpr/cstu,csu->cst/dot_general | solution.py:111
  342.3 28.5 %fusion.139 = f32[256,1,128]{2,1,0:T(1,128)S(1)} fusion(f32[256,128]{1,0:T(8,128)S(1)} %copy.93, pred[128,128]{1,0:T(8,128)(4,1)S(1)} %fusion.138, f32[8,256,1,128]{3,2,1,0:T(1,128)} %get-tuple-element.526, s32[]{:T(128)S(6)} %copy.104), kind=kOutput, calls=%fused_computation.2.clone.1 | convolution fusion | flops 62914560 | bytes 540676 | tf_op jit(solution)/shard_map/while/body/eval_jaxpr/cstu,csu->cst/dot_general | solution.py:111
  373.4 28.5 %fusion.139 = f32[256,1,128]{2,1,0:T(1,128)S(1)} fusion(f32[256,128]{1,0:T(8,128)S(1)} %copy.93, pred[128,128]{1,0:T(8,128)(4,1)S(1)} %fusion.138, f32[8,256,1,128]{3,2,1,0:T(1,128)} %get-tuple-element.526, s32[]{:T(128)S(6)} %copy.104), kind=kOutput, calls=%fused_computation.2.clone.1 | convolution fusion | flops 62914560 | bytes 540676 | tf_op jit(solution)/shard_map/while/body/eval_jaxpr/cstu,csu->cst/dot_general | solution.py:111
  407.4 19.9 %psum.49 = f32[1024]{0:T(1024)S(1)} all-reduce(f32[1024]{0:T(1024)S(1)} %bitcast.248), channel_id=1, replica_groups=mesh['dp'=4,'mp'=8] {'mp'}, use_global_device_ids=true, to_apply=%region_7.8 | all-reduce | flops 1024 | bytes 8192 | tf_op jit(solution)/shard_map/psum | solution.py:123
  461.2 127.2 %all-reduce.5.cloned.1.call-done = bf16[1024,2048]{1,0:T(8,128)(2,1)} async-done(((bf16[1024,2048]{1,0:T(8,128)(2,1)}), bf16[1024,2048]{1,0:T(8,128)(2,1)}) %all-reduce.5.cloned.1.call-update) | async-done | bytes 4194320 | tf_op jit(solution)/shard_map/psum | solution.py:129
  632.4 81.0 %reduce-scatter.9.cloned.1.call-done = bf16[128,2048]{1,0:T(8,128)(2,1)} async-done(((bf16[1024,2048]{1,0:T(8,128)(2,1)}), bf16[128,2048]{1,0:T(8,128)(2,1)}) %reduce-scatter.9.cloned.1.call-update) | async-done | bytes 524304 | tf_op jit(solution)/shard_map/reduce_scatter | solution.py:169
  734.1 56.4 %all-gather.5.cloned.1.call-done = bf16[1024,2048]{1,0:T(8,128)(2,1)} async-done(((bf16[128,2048]{1,0:T(8,128)(2,1)}), bf16[1024,2048]{1,0:T(8,128)(2,1)}) %all-gather.5.cloned.1.call-update) | async-done | bytes 4194320 | tf_op jit(solution)/shard_map/all_gather | solution.py:179
  796.0 16.6 %psum.51 = f32[1024]{0:T(1024)S(1)} all-reduce(f32[1024]{0:T(1024)S(1)} %get-tuple-element.357), channel_id=1, replica_groups=mesh['dp'=4,'mp'=8] {'mp'}, use_global_device_ids=true, to_apply=%region_16.17 | all-reduce | flops 1024 | bytes 8192 | tf_op jit(solution)/shard_map/psum | solution.py:185
  821.7 182.9 %while.33 = (s32[]{:T(128)}, f32[256,1]{0,1:T(1,128)S(1)}, f32[8,256,1,128]{1,3,2,0:T(8,128)}, f32[8,256,1]{1,2,0:T(1,128)S(1)}, f32[8,1]{0,1:T(1,128)S(1)}, /*i...) while((s32[]{:T(128)}, f32[256,1]{0,1:T(1,128)S(1)}, ...), condition=%wide.region_18.19_spmd.clone.clone, body=%wide.region_17.18_spmd.clone.clone.sunk | while | flops 113853312 | bytes 2405947 | solution.py:202
  824.8 17.7 %fusion.150 = f32[256,1,128]{2,1,0:T(1,128)S(1)} fusion(f32[256,128]{1,0:T(8,128)S(1)} %copy.95, pred[128,128]{1,0:T(8,128)(4,1)S(1)} %fusion.149, f32[8,256,1,128]{3,2,1,0:T(1,128)} %get-tuple-element.557, s32[]{:T(128)S(6)} %sub.285), kind=kOutput, calls=%fused_computation.30.clone.1 | convolution fusion | flops 62914560 | bytes 540676 | tf_op jit(solution)/shard_map/while/body/eval_jaxpr/cstu,cst->csu/dot_general | solution.py:197
  847.6 17.7 %fusion.150 = f32[256,1,128]{2,1,0:T(1,128)S(1)} fusion(f32[256,128]{1,0:T(8,128)S(1)} %copy.95, pred[128,128]{1,0:T(8,128)(4,1)S(1)} %fusion.149, f32[8,256,1,128]{3,2,1,0:T(1,128)} %get-tuple-element.557, s32[]{:T(128)S(6)} %sub.285), kind=kOutput, calls=%fused_computation.30.clone.1 | convolution fusion | flops 62914560 | bytes 540676 | tf_op jit(solution)/shard_map/while/body/eval_jaxpr/cstu,cst->csu/dot_general | solution.py:197
  870.4 17.7 %fusion.150 = f32[256,1,128]{2,1,0:T(1,128)S(1)} fusion(f32[256,128]{1,0:T(8,128)S(1)} %copy.95, pred[128,128]{1,0:T(8,128)(4,1)S(1)} %fusion.149, f32[8,256,1,128]{3,2,1,0:T(1,128)} %get-tuple-element.557, s32[]{:T(128)S(6)} %sub.285), kind=kOutput, calls=%fused_computation.30.clone.1 | convolution fusion | flops 62914560 | bytes 540676 | tf_op jit(solution)/shard_map/while/body/eval_jaxpr/cstu,cst->csu/dot_general | solution.py:197
  893.3 17.7 %fusion.150 = f32[256,1,128]{2,1,0:T(1,128)S(1)} fusion(f32[256,128]{1,0:T(8,128)S(1)} %copy.95, pred[128,128]{1,0:T(8,128)(4,1)S(1)} %fusion.149, f32[8,256,1,128]{3,2,1,0:T(1,128)} %get-tuple-element.557, s32[]{:T(128)S(6)} %sub.285), kind=kOutput, calls=%fused_computation.30.clone.1 | convolution fusion | flops 62914560 | bytes 540676 | tf_op jit(solution)/shard_map/while/body/eval_jaxpr/cstu,cst->csu/dot_general | solution.py:197
  916.1 17.7 %fusion.150 = f32[256,1,128]{2,1,0:T(1,128)S(1)} fusion(f32[256,128]{1,0:T(8,128)S(1)} %copy.95, pred[128,128]{1,0:T(8,128)(4,1)S(1)} %fusion.149, f32[8,256,1,128]{3,2,1,0:T(1,128)} %get-tuple-element.557, s32[]{:T(128)S(6)} %sub.285), kind=kOutput, calls=%fused_computation.30.clone.1 | convolution fusion | flops 62914560 | bytes 540676 | tf_op jit(solution)/shard_map/while/body/eval_jaxpr/cstu,cst->csu/dot_general | solution.py:197
  938.9 17.7 %fusion.150 = f32[256,1,128]{2,1,0:T(1,128)S(1)} fusion(f32[256,128]{1,0:T(8,128)S(1)} %copy.95, pred[128,128]{1,0:T(8,128)(4,1)S(1)} %fusion.149, f32[8,256,1,128]{3,2,1,0:T(1,128)} %get-tuple-element.557, s32[]{:T(128)S(6)} %sub.285), kind=kOutput, calls=%fused_computation.30.clone.1 | convolution fusion | flops 62914560 | bytes 540676 | tf_op jit(solution)/shard_map/while/body/eval_jaxpr/cstu,cst->csu/dot_general | solution.py:197
  961.7 17.7 %fusion.150 = f32[256,1,128]{2,1,0:T(1,128)S(1)} fusion(f32[256,128]{1,0:T(8,128)S(1)} %copy.95, pred[128,128]{1,0:T(8,128)(4,1)S(1)} %fusion.149, f32[8,256,1,128]{3,2,1,0:T(1,128)} %get-tuple-element.557, s32[]{:T(128)S(6)} %sub.285), kind=kOutput, calls=%fused_computation.30.clone.1 | convolution fusion | flops 62914560 | bytes 540676 | tf_op jit(solution)/shard_map/while/body/eval_jaxpr/cstu,cst->csu/dot_general | solution.py:197
  984.5 17.7 %fusion.150 = f32[256,1,128]{2,1,0:T(1,128)S(1)} fusion(f32[256,128]{1,0:T(8,128)S(1)} %copy.95, pred[128,128]{1,0:T(8,128)(4,1)S(1)} %fusion.149, f32[8,256,1,128]{3,2,1,0:T(1,128)} %get-tuple-element.557, s32[]{:T(128)S(6)} %sub.285), kind=kOutput, calls=%fused_computation.30.clone.1 | convolution fusion | flops 62914560 | bytes 540676 | tf_op jit(solution)/shard_map/while/body/eval_jaxpr/cstu,cst->csu/dot_general | solution.py:197
  1062.6 46.3 %reduce-scatter.11.cloned.1.call-done = bf16[128,2048]{1,0:T(8,128)(2,1)} async-done(((bf16[1024,2048]{1,0:T(8,128)(2,1)}), bf16[128,2048]{1,0:T(8,128)(2,1)}) %reduce-scatter.11.cloned.1.call-update) | async-done | bytes 524304 | tf_op jit(solution)/shard_map/reduce_scatter | solution.py:227
  1110.3 42.5 %all-reduce.1 = (f32[2048]{0:T(1024)}, f32[2048]{0:T(1024)}, f32[2048]{0:T(1024)}) all-reduce(f32[2048]{0:T(1024)S(1)} %get-tuple-element.358, f32[2048]{0:T(1024)S(1)} %get-tuple-element.354, f32[2048]{0:T(1024)S(1)} %mul.520), channel_id=1, replica_groups=mesh['dp'=4,'mp'=8] {'dp','mp'}, use_global_device_ids=true, to_apply=%region_22.23 | all-reduce | flops 6144 | bytes 49152 | tf_op jit(solution)/shard_map/psum | solution.py:259
  1152.8 48.6 %reduce-scatter.7.cloned.1.call-done = bf16[128,2048]{1,0:T(8,128)(2,1)} async-done(((bf16[1024,2048]{1,0:T(8,128)(2,1)}), bf16[128,2048]{1,0:T(8,128)(2,1)}) %reduce-scatter.7.cloned.1.call-update) | async-done | bytes 524304 | tf_op jit(solution)/shard_map/reduce_scatter | solution.py:140
  1205.0 72.9 %reduce-scatter.13.cloned.1.call-done = bf16[512,2176]{0,1:T(8,128)(2,1)} async-done(((bf16[2048,2176]{0,1:T(8,128)(2,1)}), bf16[512,2176]{0,1:T(8,128)(2,1)}) %reduce-scatter.13.cloned.1.call-update) | async-done | bytes 2228240 | tf_op jit(solution)/shard_map/reduce_scatter | solution.py:241
  1287.6 123.0 %all-reduce.7.cloned.1.call-done = f32[24,2048]{1,0:T(8,128)} async-done(((f32[24,2048]{1,0:T(8,128)}), f32[24,2048]{1,0:T(8,128)}) %all-reduce.7.cloned.1.call-update) | async-done | bytes 196624 | tf_op jit(solution)/shard_map/psum | solution.py:259
  (414 shorter events, 325.3 us)
Async XLA Ops:
  7.2 599.3 %copy-start = (bf16[704,2048]{1,0:T(8,128)(2,1)S(1)}, bf16[704,2048]{1,0:T(8,128)(2,1)}, u32[]{:S(2)}) copy-start(bf16[704,2048]{1,0:T(8,128)(2,1)} %param.35) | copy-start | bytes 8650756
  7.2 130.3 %all-gather.3.cloned.1.call-start = ((), (), s32[]{:S(2)}) async-start(), calls=%async_computation.6 | async-start | bytes 4718592 | tf_op jit(solution)/shard_map/all_gather | solution.py:68
  7.9 580.5 %all-reduce.5.cloned.1.call-start = ((), (), s32[]{:S(2)}) async-start(), calls=%async_computation.7 | async-start | bytes 8388608 | tf_op jit(solution)/shard_map/psum | solution.py:129
  8.0 15.6 %collective-permute-start = (bf16[128,2048]{1,0:T(8,128)(2,1)}, bf16[128,2048]{1,0:T(8,128)(2,1)S(1)}, u32[]{:S(2)}, u32[]{:S(2)}) collective-permute-start(bf16[128,2048]{1,0:T(8,128)(2,1)} %param.21), channel_id=1, source_target_pairs={{0,1},{1,2},{2,3},{3,4},{4,5},{5,6},{6,7},{7,0},{8,9},{9,10},{10,1... | collective-permute-start | bytes 1572872 | tf_op jit(solution)/shard_map/ppermute | solution.py:152
  24.3 26.0 %collective-permute-start.1 = (bf16[128,2048]{1,0:T(8,128)(2,1)S(1)}, bf16[128,2048]{1,0:T(8,128)(2,1)S(1)}, u32[]{:S(2)}, u32[]{:S(2)}) collective-permute-start(bf16[128,2048]{1,0:T(8,128)(2,1)S(1)} %collective-permute-done), channel_id=1, source_target_pairs={{0,1},{1,2},{2,3},{3,4},{4,5},{5,6},{6,7},{7,0},{8,9},{9,10},{10,1... | collective-permute-start | bytes 1572872 | tf_op jit(solution)/shard_map/ppermute | solution.py:152
  50.3 77.3 %copy-start.13 = (bf16[128,2048]{1,0:T(8,128)(2,1)}, bf16[128,2048]{1,0:T(8,128)(2,1)S(1)}, u32[]{:S(2)}) copy-start(bf16[128,2048]{1,0:T(8,128)(2,1)S(1)} %collective-permute-done.1) | copy-start | bytes 1572868
  50.3 20.3 %collective-permute-start.2 = (bf16[128,2048]{1,0:T(8,128)(2,1)S(1)}, bf16[128,2048]{1,0:T(8,128)(2,1)}, u32[]{:S(2)}, u32[]{:S(2)}) collective-permute-start(bf16[128,2048]{1,0:T(8,128)(2,1)S(1)} %collective-permute-done.1), channel_id=1, source_target_pairs={{0,1},{1,2},{2,3},{3,4},{4,5},{5,6},{6,7},{7,0},{8,9},{9,10},{10,1... | collective-permute-start | bytes 1572872 | tf_op jit(solution)/shard_map/ppermute | solution.py:152
  51.3 70.4 %copy-start.28 = (f32[256]{0:T(256)}, f32[256]{0:T(256)S(1)}, u32[]{:S(2)}) copy-start(f32[256]{0:T(256)S(1)} %reduce_max.9) | copy-start | bytes 3076
  51.3 59.5 %copy-start.17 = (bf16[2048,256]{1,0:T(8,128)(2,1)S(1)}, bf16[2048,256]{1,0:T(8,128)(2,1)}, u32[]{:S(2)}) copy-start(bf16[2048,256]{1,0:T(8,128)(2,1)} %param.31) | copy-start | bytes 3145732
  52.2 71.7 %copy-start.34 = (f32[256]{0:T(256)}, f32[256]{0:T(256)S(1)}, u32[]{:S(2)}) copy-start(f32[256]{0:T(256)S(1)} %fusion.85) | copy-start | bytes 3076
  70.6 26.1 %collective-permute-start.3 = (bf16[128,2048]{1,0:T(8,128)(2,1)}, bf16[128,2048]{1,0:T(8,128)(2,1)S(1)}, u32[]{:S(2)}, u32[]{:S(2)}) collective-permute-start(bf16[128,2048]{1,0:T(8,128)(2,1)} %collective-permute-done.2), channel_id=1, source_target_pairs={{0,1},{1,2},{2,3},{3,4},{4,5},{5,6},{6,7},{7,0},{8,9},{9,10},{10,1... | collective-permute-start | bytes 1572872 | tf_op jit(solution)/shard_map/ppermute | solution.py:152
  80.5 42.7 %copy-start.36 = (f32[24]{0:T(128)}, f32[24]{0:T(128)S(1)}, u32[]{:S(2)}) copy-start(f32[24]{0:T(128)S(1)} %and_convert_fusion) | copy-start | bytes 292
  97.5 24.1 %collective-permute-start.4 = (bf16[128,2048]{1,0:T(8,128)(2,1)S(1)}, bf16[128,2048]{1,0:T(8,128)(2,1)}, u32[]{:S(2)}, u32[]{:S(2)}) collective-permute-start(bf16[128,2048]{1,0:T(8,128)(2,1)S(1)} %collective-permute-done.3), channel_id=1, source_target_pairs={{0,1},{1,2},{2,3},{3,4},{4,5},{5,6},{6,7},{7,0},{8,9},{9,10},{10,1... | collective-permute-start | bytes 1572872 | tf_op jit(solution)/shard_map/ppermute | solution.py:152
  109.5 37.1 %copy-start.32 = (f32[256]{0:T(256)}, f32[256]{0:T(256)S(1)}, u32[]{:S(2)}) copy-start(f32[256]{0:T(256)S(1)} %multiply_reduce_fusion.4) | copy-start | bytes 3076
  121.7 12.0 collective-permute-start.5
  123.9 22.7 %copy-start.30 = (f32[256]{0:T(256)}, f32[256]{0:T(256)S(1)}, u32[]{:S(2)}) copy-start(f32[256]{0:T(256)S(1)} %broadcast_subtract_fusion.1) | copy-start | bytes 3076
  123.9 16.9 %copy-start.26 = (f32[2048]{0:T(1024)S(1)}, f32[2048]{0:T(1024)}, u32[]{:S(2)}) copy-start(f32[2048]{0:T(1024)} %param.25) | copy-start | bytes 24580
  133.6 305.4 %collective-permute-start.6 = (bf16[128,2048]{1,0:T(8,128)(2,1)}, bf16[128,2048]{1,0:T(8,128)(2,1)}, u32[]{:S(2)}, u32[]{:S(2)}) collective-permute-start(bf16[128,2048]{1,0:T(8,128)(2,1)} %collective-permute-done.5), channel_id=1, source_target_pairs={{0,1},{1,2},{2,3},{3,4},{4,5},{5,6},{6,7},{7,0},{8,9},{9,10},{10,1... | collective-permute-start | bytes 1572872 | tf_op jit(solution)/shard_map/ppermute | solution.py:152
  153.5 273.8 %copy-start.40 = (f32[256]{0:T(256)S(1)}, f32[256]{0:T(256)}, u32[]{:S(2)}) copy-start(f32[256]{0:T(256)} %param.27) | copy-start | bytes 3076
  433.7 279.6 %reduce-scatter.9.cloned.1.call-start = ((), (), s32[]{:S(2)}) async-start(), calls=%async_computation.9 | async-start | bytes 4718592 | tf_op jit(solution)/shard_map/reduce_scatter | solution.py:169
  461.2 135.4 %copy-start.25 = (f32[2048]{0:T(1024)S(1)}, f32[2048]{0:T(1024)}, u32[]{:S(2)}) copy-start(f32[2048]{0:T(1024)} %param.26) | copy-start | bytes 24580
  596.7 19.3 %slice-start = ((s8[5767168]{0:T(1024)(128)(4,1)}), s8[1572864]{0:T(1024)(128)(4,1)S(1)}, s32[]{:S(2)}) async-start(s8[5767168]{0:T(1024)(128)(4,1)} %bitcast.230), calls=%async_computation.16 | async-start | bytes 3145728
  624.3 166.1 %all-gather.5.cloned.1.call-start = ((), (), s32[]{:S(2)}) async-start(), calls=%async_computation.10 | async-start | bytes 4718592 | tf_op jit(solution)/shard_map/all_gather | solution.py:179
  718.0 339.2 %reduce-scatter.17.cloned.1.call-start = ((), (), s32[]{:S(2)}) async-start(), calls=%async_computation.15 | async-start | bytes 3604480 | tf_op jit(solution)/shard_map/reduce_scatter | solution.py:251
  725.9 334.8 %reduce-scatter.15.cloned.1.call-start = ((), (), s32[]{:S(2)}) async-start(), calls=%async_computation.14 | async-start | bytes 1310720 | tf_op jit(solution)/shard_map/reduce_scatter | solution.py:248
  820.6 288.2 %reduce-scatter.11.cloned.1.call-start = ((), (), s32[]{:S(2)}) async-start(), calls=%async_computation.11 | async-start | bytes 4718592 | tf_op jit(solution)/shard_map/reduce_scatter | solution.py:227
  1020.5 180.9 %reduce-scatter.7.cloned.1.call-start = ((), (), s32[]{:S(2)}) async-start(), calls=%async_computation.8 | async-start | bytes 4718592 | tf_op jit(solution)/shard_map/reduce_scatter | solution.py:140
  1026.9 13.6 copy-start.27
  1026.9 13.6 copy-start.39
  1027.0 250.9 %reduce-scatter.13.cloned.1.call-start = ((), (), s32[]{:S(2)}) async-start(), calls=%async_computation.13 | async-start | bytes 11141120 | tf_op jit(solution)/shard_map/reduce_scatter | solution.py:241
  1027.0 13.6 copy-start.5
  1056.0 354.5 %all-reduce.7.cloned.1.call-start = ((), (), s32[]{:S(2)}) async-start(), calls=%async_computation.12 | async-start | bytes 393216 | tf_op jit(solution)/shard_map/psum | solution.py:259
  (32 other events, 173.8 us)
Sparse Core Ops, SparseCore 0:
  10.2 103.9 all-gather.2
  433.9 154.5 all-reduce.4
  624.5 88.8 reduce-scatter.8
  718.1 72.2 all-gather.4
  793.0 34.3 reduce-scatter.16
  829.7 24.8 reduce-scatter.14
  1020.6 88.2 reduce-scatter.10
  1112.5 88.8 reduce-scatter.6
  1204.2 73.6 reduce-scatter.12
  1284.8 125.7 all-reduce.6
